TPU v7x, 512 devices: a whole 4x4x16 slice. The times are simulated.
512 devices in a mesh: row: 32 (over x, z_lo), col: 16 (over y, z_hi, core).
Axes of the slice: x: 4, y: 4, z: 16 (z_hi: 2, z_lo: 8; z = z_hi * 8 + z_lo), core: 2. Of those that a mesh axis runs over, the one named last changes fastest.
Arguments:
- ancestor: float32 [12288, 12288], P('row', 'col'), may hold values from -6 to 6
- pattern: int32 [96, 96], P('row', 'col'), may hold values 0 or 1
- member: int32 [96, 2], replicated, may hold values 0 or 1
- panel: float32 [12288, 512], P('col', 'row'), may hold values from -0.0546875 to 0.0546875
- diag_inv: float32 [256, 512], P(None, 'col'), may hold values from -6 to 6
Outputs:
- ancestor_panel: float32 [12288, 512], P('row', 'col')
- diag_blocks: float32 [256, 512], P(None, 'col')
All inputs are finite; a program needn't handle non-finite values. No bound on the sum of `pattern` on one device may be relied on, other than what follows from the above.
Results may differ from a plain program's by a relative error of at most 0.0001.
Values sent between devices are 32-bit elements; how exact they have to be, the bound alone decides.
No kernel may reach another device: no remote copies, remote signals or barrier semaphores. Data moves between devices by JAX's collectives and lax.ppermute only.
A program may use at most 64 MiB of HBM per device.

v0:
```python
import jax
import jax.numpy as jnp
from jax import lax
from jax.sharding import PartitionSpec as P

W = 256
BS = 128


def spread(block, axis, owner):
    block = jnp.where(lax.axis_index(axis) == owner, block, jnp.zeros_like(block))
    return lax.psum(block, axis)


def pick_member(member, start, count, which):
    rows = lax.dynamic_slice_in_dim(member, start, count, 0).astype(jnp.float32)
    return jnp.where(which == 0, rows[:, 0], rows[:, 1])


def both_terms(normed_rows, values):
    first_term = jnp.dot(
        normed_rows[:, :W].T,
        values[:, :W],
        precision=lax.Precision.HIGHEST,
        preferred_element_type=jnp.float32,
    )
    second_term = jnp.dot(
        normed_rows[:, W:].T,
        values[:, W:],
        precision=lax.Precision.HIGHEST,
        preferred_element_type=jnp.float32,
    )
    return jnp.concatenate([first_term, second_term], axis=1)


def body(ancestor, pattern, member, panel, diag_inv):
    row_count = lax.axis_size("row")
    col_count = lax.axis_size("col")
    row_idx = lax.axis_index("row")
    col_idx = lax.axis_index("col")
    row_blocks, col_blocks = pattern.shape
    local_rows, local_cols = ancestor.shape
    slice_cols = panel.shape[1]
    panel_owner = row_idx * slice_cols // W
    chosen = pick_member(member, col_idx * col_blocks, col_blocks, panel_owner)
    masked_panel = (panel.reshape(col_blocks, BS, slice_cols) * chosen[:, None, None]).reshape(
        local_cols, slice_cols
    )
    full_cols = lax.all_gather(masked_panel, "row", axis=1, tiled=True)
    weights = pattern.astype(jnp.float32)
    masked = (ancestor.reshape(row_blocks, BS, col_blocks, BS) * weights[:, None, :, None]).reshape(
        local_rows, local_cols
    )
    partial_value = jnp.dot(
        masked, full_cols, precision=lax.Precision.HIGHEST, preferred_element_type=jnp.float32
    )
    own_cols = diag_inv.shape[1]
    own_owner = col_idx * own_cols // W
    picked = pick_member(member, row_idx * row_blocks, row_blocks, own_owner)
    keep_rows = jnp.repeat(picked, BS)
    fold_ratio = row_count // col_count
    sender = lax.dynamic_slice_in_dim(full_cols, row_idx % fold_ratio * local_rows, local_rows, 0)
    summed = lax.psum_scatter(partial_value, "col", scatter_dimension=1, tiled=True)
    ancestor_panel = -(summed * keep_rows[:, None])
    normed_rows = spread(sender, "col", row_idx // fold_ratio)
    block_term = both_terms(normed_rows, partial_value)
    totals = lax.psum(block_term, ("row", "col"))
    diag_out = diag_inv + lax.dynamic_slice_in_dim(totals, col_idx * own_cols, own_cols, 1)
    return (ancestor_panel, diag_out)


def solution(mesh):
    placed = (P("row", "col"), P("row", "col"), P(), P("col", "row"), P(None, "col"))
    return jax.shard_map(
        body,
        mesh=mesh,
        in_specs=placed,
        out_specs=(P("row", "col"), P(None, "col")),
        check_vma=False,
    )
```

profile of v0, /device:TPU:2, one launch (start us, length us, event | category | flops | bytes accessed | tf_op | source)
XLA Modules:
  0.0 1086.8 jit_solution(8966737498046524540)
XLA Ops:
  7.2 0.0 copy-start.4
  7.2 0.0 all-gather.2.cloned.1.call-start
  7.2 0.8 dynamic-slice_convert_fusion.1
  8.0 0.1 broadcast_bitcast_fusion
  8.1 1.4 broadcast_multiply_fusion
  9.5 0.0 all-gather.2.cloned.1.call-update
  9.5 0.0 all-reduce.3.cloned.1.call-start
  9.6 212.4 %all-gather.2.cloned.1.call-done = f32[768,512]{0,1:T(8,128)} async-done(((f32[768,16]{0,1:T(8,128)}), f32[768,512]{0,1:T(8,128)}) %all-gather.2.cloned.1.call-update) | async-done | bytes 1572880 | tf_op jit(solution)/shard_map/all_gather | solution.py:49
  222.0 0.0 copy-start.1
  222.0 2.2 dynamic-slice_select_fusion
  224.2 0.0 copy-start
  224.2 0.0 all-reduce.3.cloned.1.call-update
  224.2 0.0 all-reduce.5.cloned.1.call-start
  224.2 0.0 copy-done.4
  224.3 0.2 mul.50
  224.4 0.0 copy-done.1
  224.5 1.1 copy-done
  225.6 2.2 fusion
  227.8 273.9 %all-reduce.3.cloned.1.call-done = f32[384,512]{0,1:T(8,128)} async-done(((f32[384,512]{0,1:T(8,128)}), f32[384,512]{0,1:T(8,128)}) %all-reduce.3.cloned.1.call-update) | async-done | bytes 786448 | tf_op jit(solution)/shard_map/psum | solution.py:12
  501.7 1.8 fusion.2
  503.5 1.8 fusion.5
  505.3 0.8 pad_maximum_fusion
  506.1 0.0 copy-start.3
  506.1 0.0 copy-start.2
  506.1 0.0 all-reduce.5.cloned.1.call-update
  506.2 0.0 reduce-scatter.4.cloned.1.call-start
  506.2 1.2 copy.10
  507.4 0.0 reduce-scatter.4.cloned.1.call-update
  507.4 0.0 copy-done.3
  507.4 0.1 dynamic-slice_convert_fusion
  507.5 0.1 broadcast_bitcast_fusion.1
  507.6 466.2 %all-reduce.5.cloned.1.call-done = f32[256,512]{0,1:T(8,128)} async-done(((f32[256,512]{0,1:T(8,128)}), f32[256,512]{0,1:T(8,128)}) %all-reduce.5.cloned.1.call-update) | async-done | bytes 524304 | tf_op jit(solution)/shard_map/psum | solution.py:67
  973.8 0.0 copy-done.2
  973.8 1.4 dynamic-slice_add_fusion
  975.2 103.2 %reduce-scatter.4.cloned.1.call-done = f32[32,384]{1,0:T(8,128)} async-done(((f32[512,384]{1,0:T(8,128)}), f32[32,384]{1,0:T(8,128)}) %reduce-scatter.4.cloned.1.call-update) | async-done | bytes 49168
  1078.4 0.9 copy.11
  1079.4 0.1 multiply_negate_fusion
  1079.5 0.7 copy.9
  (3 shorter events, 0.0 us)
Async XLA Ops:
  7.2 217.1 %copy-start.4 = (s32[3,6]{1,0:T(4,128)S(1)}, s32[3,6]{1,0:T(4,128)}, u32[]{:S(2)}) copy-start(s32[3,6]{1,0:T(4,128)} %param.6) | copy-start | bytes 220
  7.2 214.8 %all-gather.2.cloned.1.call-start = ((), (), s32[]{:S(2)}) async-start(), calls=%async_computation.1 | async-start | bytes 1622016 | tf_op jit(solution)/shard_map/all_gather | solution.py:49
  9.5 492.2 %all-reduce.3.cloned.1.call-start = ((), (), s32[]{:S(2)}) async-start(), calls=%async_computation.2 | async-start | bytes 1572864 | tf_op jit(solution)/shard_map/psum | solution.py:12
  222.0 2.4 copy-start.1
  224.2 1.4 copy-start
  224.2 749.6 %all-reduce.5.cloned.1.call-start = ((), (), s32[]{:S(2)}) async-start(), calls=%async_computation.3 | async-start | bytes 1048576 | tf_op jit(solution)/shard_map/psum | solution.py:67
  506.1 1.3 copy-start.3
  506.1 467.7 %copy-start.2 = (f32[256,32]{0,1:T(8,128)S(1)}, f32[256,32]{0,1:T(8,128)}, u32[]{:S(2)}) copy-start(f32[256,32]{0,1:T(8,128)} %param.9) | copy-start | bytes 98308
  506.2 572.3 %reduce-scatter.4.cloned.1.call-start = ((), (), s32[]{:S(2)}) async-start(), calls=%async_computation.4 | async-start | bytes 835584
Sparse Core Ops, SparseCore 0:
  10.6 211.3 all-gather.1
  224.9 276.7 all-reduce.2
  507.1 466.6 all-reduce.4
  978.3 100.0 reduce-scatter.3
where the time goes:
time: 1090 us
  waiting for transfers between devices  1060 us (97%)
  between operations  13.9 us (1%)
    psum x1, waiting for transfers between devices, body(): totals = lax.psum(block_term, ('row', 'col'))  466 us
    psum x1, waiting for transfers between devices, spread(): return lax.psum(block, axis)  274 us
    all_gather x1, waiting for transfers between devices, body(): full_cols = lax.all_gather(masked_panel, 'row', axis=1, tiled=True)  212 us
    unnamed x5, waiting for transfers between devices  103 us
  transfers between devices with their start and end apart: 4, of which 4 were waited for; matrix products, arithmetic and copies ran while one was open for 0% of the time, Pallas kernels for 0%

commit v1 on v0

--- a/solution.py
+++ b/solution.py
@@ -64,7 +64,7 @@
     ancestor_panel = -(summed * keep_rows[:, None])
     normed_rows = spread(sender, "col", row_idx // fold_ratio)
     block_term = both_terms(normed_rows, partial_value)
-    totals = lax.psum(block_term, ("row", "col"))
+    totals = lax.psum(lax.psum(block_term, "row"), "col")
     diag_out = diag_inv + lax.dynamic_slice_in_dim(totals, col_idx * own_cols, own_cols, 1)
     return (ancestor_panel, diag_out)
 

time: 1090 us -> 1330 us (1.22)
  the two profiles are of different devices: /device:TPU:2 before, /device:TPU:1 now
where the time goes in v1:
time: 1330 us
  waiting for transfers between devices  1300 us (98%)
  between operations  13.9 us (1%)
    psum x2, waiting for transfers between devices, body(): totals = lax.psum(lax.psum(block_term, 'row'), 'col')  683 us
    psum x1, waiting for transfers between devices, spread(): return lax.psum(block, axis)  278 us
    all_gather x1, waiting for transfers between devices, body(): full_cols = lax.all_gather(masked_panel, 'row', axis=1, tiled=True)  209 us
    unnamed x6, waiting for transfers between devices  129 us
  transfers between devices with their start and end apart: 5, of which 5 were waited for; matrix products, arithmetic and copies ran while one was open for 0% of the time, Pallas kernels for 0%

profile of v1, /device:TPU:1, one launch (start us, length us, event | category | flops | bytes accessed | tf_op | source)
XLA Modules:
  0.0 1329.3 jit_solution(442735773035054687)
XLA Ops:
  7.2 0.0 copy-start.4
  7.2 0.0 all-gather.2.cloned.1.call-start
  7.2 0.8 dynamic-slice_convert_fusion.1
  8.0 0.1 broadcast_bitcast_fusion
  8.1 1.4 broadcast_multiply_fusion
  9.5 0.0 all-gather.2.cloned.1.call-update
  9.5 0.0 all-reduce.4.cloned.1.call-start
  9.6 208.7 %all-gather.2.cloned.1.call-done = f32[768,512]{0,1:T(8,128)} async-done(((f32[768,16]{0,1:T(8,128)}), f32[768,512]{0,1:T(8,128)}) %all-gather.2.cloned.1.call-update) | async-done | bytes 1572880 | tf_op jit(solution)/shard_map/all_gather | solution.py:49
  218.3 0.0 copy-start.1
  218.3 2.2 dynamic-slice_select_fusion
  220.4 0.0 copy-start
  220.4 0.0 all-reduce.4.cloned.1.call-update
  220.5 0.0 all-reduce.6.cloned.1.call-start
  220.5 0.0 copy-done.4
  220.5 0.2 mul.50
  220.7 0.0 copy-done.1
  220.7 1.1 copy-done
  221.8 2.2 fusion
  224.0 278.2 %all-reduce.4.cloned.1.call-done = f32[384,512]{0,1:T(8,128)} async-done(((f32[384,512]{0,1:T(8,128)}), f32[384,512]{0,1:T(8,128)}) %all-reduce.4.cloned.1.call-update) | async-done | bytes 786448 | tf_op jit(solution)/shard_map/psum | solution.py:12
  502.2 1.8 fusion.2
  504.0 1.8 fusion.5
  505.8 0.8 pad_maximum_fusion
  506.7 0.0 copy-start.3
  506.7 0.0 all-reduce.6.cloned.1.call-update
  506.7 0.0 copy-start.2
  506.7 0.0 reduce-scatter.4.cloned.1.call-start
  506.7 1.2 copy.10
  507.9 0.0 reduce-scatter.4.cloned.1.call-update
  507.9 0.0 all-reduce.8.cloned.1.call-start
  508.0 0.0 copy-done.3
  508.0 0.1 dynamic-slice_convert_fusion
  508.1 432.0 %all-reduce.6.cloned.1.call-done = f32[256,512]{0,1:T(8,128)} async-done(((f32[256,512]{0,1:T(8,128)}), f32[256,512]{0,1:T(8,128)}) %all-reduce.6.cloned.1.call-update) | async-done | bytes 524304 | tf_op jit(solution)/shard_map/psum | solution.py:67
  940.1 0.0 all-reduce.8.cloned.1.call-update
  940.1 0.1 broadcast_bitcast_fusion.1
  940.2 128.4 %reduce-scatter.4.cloned.1.call-done = f32[32,384]{1,0:T(8,128)} async-done(((f32[512,384]{1,0:T(8,128)}), f32[32,384]{1,0:T(8,128)}) %reduce-scatter.4.cloned.1.call-update) | async-done | bytes 49168
  1068.6 0.9 copy.11
  1069.6 0.1 multiply_negate_fusion
  1069.7 0.7 copy.9
  1070.4 250.9 %all-reduce.8.cloned.1.call-done = f32[256,512]{0,1:T(8,128)} async-done(((f32[256,512]{0,1:T(8,128)}), f32[256,512]{0,1:T(8,128)}) %all-reduce.8.cloned.1.call-update) | async-done | bytes 524304 | tf_op jit(solution)/shard_map/psum | solution.py:67
  1321.3 0.0 copy-done.2
  1321.4 1.4 dynamic-slice_add_fusion
  (3 shorter events, 0.0 us)
Async XLA Ops:
  7.2 213.3 %copy-start.4 = (s32[3,6]{1,0:T(4,128)S(1)}, s32[3,6]{1,0:T(4,128)}, u32[]{:S(2)}) copy-start(s32[3,6]{1,0:T(4,128)} %param.6) | copy-start | bytes 220
  7.2 211.1 %all-gather.2.cloned.1.call-start = ((), (), s32[]{:S(2)}) async-start(), calls=%async_computation.1 | async-start | bytes 1622016 | tf_op jit(solution)/shard_map/all_gather | solution.py:49
  9.5 492.7 %all-reduce.4.cloned.1.call-start = ((), (), s32[]{:S(2)}) async-start(), calls=%async_computation.2 | async-start | bytes 1572864 | tf_op jit(solution)/shard_map/psum | solution.py:12
  218.3 2.4 copy-start.1
  220.4 1.4 copy-start
  220.5 719.6 %all-reduce.6.cloned.1.call-start = ((), (), s32[]{:S(2)}) async-start(), calls=%async_computation.3 | async-start | bytes 1048576 | tf_op jit(solution)/shard_map/psum | solution.py:67
  506.7 1.3 copy-start.3
  506.7 814.7 %copy-start.2 = (f32[256,32]{0,1:T(8,128)S(1)}, f32[256,32]{0,1:T(8,128)}, u32[]{:S(2)}) copy-start(f32[256,32]{0,1:T(8,128)} %param.9) | copy-start | bytes 98308
  506.7 562.0 %reduce-scatter.4.cloned.1.call-start = ((), (), s32[]{:S(2)}) async-start(), calls=%async_computation.5 | async-start | bytes 835584
  507.9 813.4 %all-reduce.8.cloned.1.call-start = ((), (), s32[]{:S(2)}) async-start(), calls=%async_computation.4 | async-start | bytes 1048576 | tf_op jit(solution)/shard_map/psum | solution.py:67
Sparse Core Ops, SparseCore 0:
  10.6 207.5 all-gather.1
  221.2 281.0 all-reduce.3
  506.8 433.2 all-reduce.5
  944.6 124.0 reduce-scatter.3
  1071.4 249.9 all-reduce.7
